TPU v7x, 32 devices: a whole 2x2x4 slice. The times are simulated.
32 devices in a mesh: dp: 8 (over z, x), th: 2 (over core), tw: 2 (over y).
Axes of the slice: x: 2, y: 2, z: 4, core: 2. Of those that a mesh axis runs over, the one named last changes fastest.
Arguments:
- tokens: bfloat16 [16, 1536, 768], P('dp', ('th', 'tw')), may hold values from -6 to 6
- segment_ids: int32 [16, 1536], P('dp'), may hold values from 0 to 7, never falling along the last dimension, each value on 1 to 768 neighbouring positions
- norm1_gain: float32 [768], replicated, may hold values from 0.5 to 1.5
- norm1_shift: float32 [768], replicated, may hold values from -3 to 3
- w_qkv: bfloat16 [3, 768, 768], P(None, None, ('th', 'tw')), may hold values from -0.21875 to 0.21875
- b_qv: float32 [2, 768], P(None, ('th', 'tw')), may hold values from -3 to 3
- w_out: bfloat16 [768, 768], P(('th', 'tw')), may hold values from -0.875 to 0.875
- b_out: float32 [768], replicated, may hold values from -3 to 3
- norm2_gain: float32 [768], replicated, may hold values from 0.5 to 1.5
- norm2_shift: float32 [768], replicated, may hold values from -3 to 3
- w_up: bfloat16 [768, 3072], replicated, may hold values from -0.21875 to 0.21875
- b_up: float32 [3072], replicated, may hold values from -3 to 3
- w_down: bfloat16 [3072, 768], replicated, may hold values from -0.109375 to 0.109375
- b_down: float32 [768], replicated, may hold values from -3 to 3
- cotangent: bfloat16 [16, 1536, 768], P('dp', ('th', 'tw')), may hold values from -6 to 6
Outputs:
- block_out: bfloat16 [16, 1536, 768], P('dp', ('th', 'tw'))
- grad_tokens: bfloat16 [16, 1536, 768], P('dp', ('th', 'tw'))
- grad_norm1_gain: float32 [768], replicated
- grad_norm1_shift: float32 [768], replicated
- grad_w_qkv: float32 [3, 768, 768], P(None, None, ('th', 'tw'))
- grad_b_qv: float32 [2, 768], P(None, ('th', 'tw'))
- grad_w_out: float32 [768, 768], P(('th', 'tw'))
- grad_b_out: float32 [768], replicated
- grad_norm2_gain: float32 [768], replicated
- grad_norm2_shift: float32 [768], replicated
- grad_w_up: float32 [768, 3072], replicated
- grad_b_up: float32 [3072], replicated
- grad_w_down: float32 [3072, 768], replicated
- grad_b_down: float32 [768], replicated
Inputs may be any that keep to these rules, and one draw needn't show every extreme that they name: `segment_ids`: within each row the ids never fall, and one image holds 1 to 768 tokens.
All inputs are finite; a program needn't handle non-finite values.
Results may differ from a plain program's by a relative error of at most 0.015.
Values may be sent and summed in bfloat16 or wider, within the bound.
A program may use at most 192 MiB of HBM per device.

v0:
```python
import jax
import jax.numpy as jnp
from jax import lax
from jax.sharding import PartitionSpec as P

HD = 64
EPSILON = 1e-06


def layer_norm(field, norm_gain, norm_shift):
    average = jnp.mean(field, axis=-1, keepdims=True)
    centred = field - average
    spread = jnp.mean(centred * centred, axis=-1, keepdims=True)
    return centred * lax.rsqrt(spread + EPSILON) * norm_gain + norm_shift


def gelu_exact(field):
    return jax.nn.gelu(field, approximate=False)


def masked_scores(query_block, key_rows, row_seg, offset, block_rows):
    score_scale = query_block.shape[-1] ** (-0.5)
    same_image = row_seg[offset : offset + block_rows, None] == row_seg[None, :]
    scores = (
        jnp.einsum("qhe,khe->hqk", query_block, key_rows, preferred_element_type=jnp.float32)
        * score_scale
    )
    return jnp.where(same_image[None], scores, -1000000000.0)


def row_forward(row_items):
    row_qkv, row_seg = row_items
    length = row_qkv.shape[1]
    head_count = row_qkv.shape[2] // HD
    key_rows = row_qkv[1].reshape(length, head_count, HD)
    value_rows = row_qkv[2].reshape(length, head_count, HD)
    block_rows = min(512, length)
    head_outs = []
    log_totals = []
    for offset in range(0, length, block_rows):
        query_block = row_qkv[0, offset : offset + block_rows].reshape(block_rows, head_count, HD)
        scores = masked_scores(query_block, key_rows, row_seg, offset, block_rows)
        row_peak = jnp.max(scores, axis=-1, keepdims=True)
        exponent = jnp.exp(scores - row_peak)
        denominator = jnp.sum(exponent, axis=-1, keepdims=True)
        weights_low = (exponent / denominator).astype(jnp.bfloat16)
        head_out = jnp.einsum(
            "hqk,khe->qhe", weights_low, value_rows, preferred_element_type=jnp.float32
        )
        head_outs.append(head_out.reshape(block_rows, head_count * HD).astype(jnp.bfloat16))
        log_totals.append((row_peak + jnp.log(denominator))[..., 0])
    return (jnp.concatenate(head_outs, 0), jnp.concatenate(log_totals, 1))


def row_backward(row_items):
    row_qkv, row_grad, row_total, row_seg = row_items
    length = row_qkv.shape[1]
    head_count = row_qkv.shape[2] // HD
    score_scale = HD ** (-0.5)
    key_rows = row_qkv[1].reshape(length, head_count, HD)
    value_rows = row_qkv[2].reshape(length, head_count, HD)
    block_rows = min(512, length)
    key_grad = jnp.zeros((length, head_count, HD), jnp.float32)
    value_grad = jnp.zeros((length, head_count, HD), jnp.float32)
    query_grads = []
    for offset in range(0, length, block_rows):
        query_block = row_qkv[0, offset : offset + block_rows].reshape(block_rows, head_count, HD)
        upstream = row_grad[offset : offset + block_rows].reshape(block_rows, head_count, HD)
        scores = masked_scores(query_block, key_rows, row_seg, offset, block_rows)
        probability = jnp.exp(scores - row_total[:, offset : offset + block_rows, None])
        value_grad = value_grad + jnp.einsum(
            "hqk,qhe->khe",
            probability.astype(jnp.bfloat16),
            upstream,
            preferred_element_type=jnp.float32,
        )
        prob_grad = jnp.einsum(
            "qhe,khe->hqk", upstream, value_rows, preferred_element_type=jnp.float32
        )
        row_inner = jnp.sum(probability * prob_grad, axis=-1, keepdims=True)
        score_grad = (probability * (prob_grad - row_inner)).astype(jnp.bfloat16) * score_scale
        query_grad = jnp.einsum(
            "hqk,khe->qhe", score_grad, key_rows, preferred_element_type=jnp.float32
        )
        query_grads.append(query_grad.reshape(block_rows, head_count * HD))
        key_grad = key_grad + jnp.einsum(
            "hqk,qhe->khe", score_grad, query_block, preferred_element_type=jnp.float32
        )
    stacked = jnp.stack(
        [
            jnp.concatenate(query_grads, 0),
            key_grad.reshape(length, head_count * HD),
            value_grad.reshape(length, head_count * HD),
        ]
    )
    return stacked.astype(jnp.bfloat16)


def body(
    tokens,
    segment_ids,
    norm1_gain,
    norm1_shift,
    w_qkv,
    b_qv,
    w_out,
    b_out,
    norm2_gain,
    norm2_shift,
    w_up,
    b_up,
    w_down,
    b_down,
    cotangent,
):
    inputs = tokens.astype(jnp.float32)
    normed_one, norm_one_back = jax.vjp(layer_norm, inputs, norm1_gain, norm1_shift)
    normed_low = normed_one.astype(jnp.bfloat16)
    gathered = lax.all_gather(normed_low, ("th", "tw"), axis=1, tiled=True)
    bias_rows = jnp.stack([b_qv[0], jnp.zeros_like(b_qv[0]), b_qv[1]])
    projected = jnp.einsum("rld,cde->rcle", gathered, w_qkv, preferred_element_type=jnp.float32)
    projected_low = (projected + bias_rows[None, :, None, :]).astype(jnp.bfloat16)
    heads_out, totals = lax.map(row_forward, (projected_low, segment_ids))
    partial_out = jnp.einsum("rle,ed->rld", heads_out, w_out, preferred_element_type=jnp.float32)
    branch = (
        lax.psum_scatter(
            partial_out.astype(jnp.bfloat16), ("th", "tw"), scatter_dimension=1, tiled=True
        ).astype(jnp.float32)
        + b_out
    )
    middle = inputs + branch
    normed_two, norm_two_back = jax.vjp(layer_norm, middle, norm2_gain, norm2_shift)
    second_low = normed_two.astype(jnp.bfloat16)
    hidden_pre = (
        jnp.einsum("rld,df->rlf", second_low, w_up, preferred_element_type=jnp.float32) + b_up
    )
    activated, gelu_back = jax.vjp(gelu_exact, hidden_pre)
    active_low = activated.astype(jnp.bfloat16)
    block_out = middle + (
        jnp.einsum("rlf,fd->rld", active_low, w_down, preferred_element_type=jnp.float32) + b_down
    )
    upstream = cotangent.astype(jnp.float32)
    grad_w_down = jnp.einsum(
        "rlf,rld->fd", active_low, cotangent, preferred_element_type=jnp.float32
    )
    grad_b_down = jnp.sum(upstream, axis=(0, 1))
    grad_active = jnp.einsum("rld,fd->rlf", cotangent, w_down, preferred_element_type=jnp.float32)
    grad_hidden = gelu_back(grad_active)[0].astype(jnp.bfloat16)
    grad_w_up = jnp.einsum(
        "rld,rlf->df", second_low, grad_hidden, preferred_element_type=jnp.float32
    )
    grad_b_up = jnp.sum(grad_hidden.astype(jnp.float32), axis=(0, 1))
    grad_normed_two = jnp.einsum(
        "rlf,df->rld", grad_hidden, w_up, preferred_element_type=jnp.float32
    )
    grad_mid_norm, grad_gain_two, grad_shift_two = norm_two_back(grad_normed_two)
    grad_middle = upstream + grad_mid_norm
    grad_branch = grad_middle.astype(jnp.bfloat16)
    grad_b_out = jnp.sum(grad_branch.astype(jnp.float32), axis=(0, 1))
    grad_whole = lax.all_gather(grad_branch, ("th", "tw"), axis=1, tiled=True)
    grad_heads = jnp.einsum(
        "rld,ed->rle", grad_whole, w_out, preferred_element_type=jnp.float32
    ).astype(jnp.bfloat16)
    grad_w_out = jnp.einsum(
        "rle,rld->ed", heads_out, grad_whole, preferred_element_type=jnp.float32
    )
    grad_qkv = lax.map(row_backward, (projected_low, grad_heads, totals, segment_ids))
    grad_w_qkv = jnp.einsum("rld,rcle->cde", gathered, grad_qkv, preferred_element_type=jnp.float32)
    grad_b_qv = jnp.sum(grad_qkv[:, 0::2].astype(jnp.float32), axis=(0, 2))
    grad_normed = jnp.einsum("rcle,cde->rld", grad_qkv, w_qkv, preferred_element_type=jnp.float32)
    grad_tile = lax.psum_scatter(
        grad_normed.astype(jnp.bfloat16), ("th", "tw"), scatter_dimension=1, tiled=True
    ).astype(jnp.float32)
    grad_inputs, grad_gain_one, grad_shift_one = norm_one_back(grad_tile)
    grad_tokens = (grad_middle + grad_inputs).astype(jnp.bfloat16)
    head_sums = (
        lax.psum(grad_w_qkv.astype(jnp.bfloat16), "dp").astype(jnp.float32),
        lax.psum(grad_b_qv.astype(jnp.bfloat16), "dp").astype(jnp.float32),
        lax.psum(grad_w_out.astype(jnp.bfloat16), "dp").astype(jnp.float32),
    )
    shared = lax.psum(
        (
            grad_gain_one,
            grad_shift_one,
            grad_b_out,
            grad_gain_two,
            grad_shift_two,
            grad_w_up,
            grad_b_up,
            grad_w_down,
            grad_b_down,
        ),
        ("dp", "th", "tw"),
    )
    return (
        block_out.astype(jnp.bfloat16),
        grad_tokens,
        shared[0],
        shared[1],
        head_sums[0],
        head_sums[1],
        head_sums[2],
        shared[2],
        shared[3],
        shared[4],
        shared[5],
        shared[6],
        shared[7],
        shared[8],
    )


def solution(mesh):
    return jax.shard_map(
        body,
        mesh=mesh,
        in_specs=(
            P("dp", ("th", "tw"), None),
            P("dp", None),
            P(),
            P(),
            P(None, None, ("th", "tw")),
            P(None, ("th", "tw")),
            P(("th", "tw"), None),
            P(),
            P(),
            P(),
            P(),
            P(),
            P(),
            P(),
            P("dp", ("th", "tw"), None),
        ),
        out_specs=(
            P("dp", ("th", "tw"), None),
            P("dp", ("th", "tw"), None),
            P(),
            P(),
            P(None, None, ("th", "tw")),
            P(None, ("th", "tw")),
            P(("th", "tw"), None),
            P(),
            P(),
            P(),
            P(),
            P(),
            P(),
            P(),
        ),
        check_vma=False,
    )
```

profile of v0, /device:TPU:0, one launch (start us, length us, event | category | flops | bytes accessed | tf_op | source)
XLA Modules:
  0.0 1006.1 jit_solution(13144696597506998621)
XLA Ops:
  11.7 2.8 fusion.160
  14.8 40.1 %all-gather.3.cloned.1.call-done = bf16[2,1536,768]{2,1,0:T(8,128)(2,1)} async-done(((bf16[2,384,768]{2,1,0:T(8,128)(2,1)}), bf16[2,1536,768]{2,1,0:T(8,128)(2,1)}) %all-gather.3.cloned.1.call-update) | async-done | bytes 4718608 | tf_op jit(solution)/shard_map/all_gather | solution.py:119
  54.9 6.7 fusion.154
  61.6 59.3 %while.22 = (s32[]{:T(128)}, bf16[2,1536,192]{1,2,0:T(8,128)(2,1)S(1)}, f32[2,3,1536]{2,1,0:T(4,128)S(1)}, bf16[2,3,1536,192]{2,3,1,0:T(8,128)(2,1)}, s32[2,1536...) while((s32[]{:T(128)}, bf16[2,1536,192]{1,2,0:T(8,128)(2,1)S(1)}, ...), condition=%wide.region_9.10_spmd, body=%wide.region_2.9_spmd.sunk | while | flops 1901302272 | bytes 107581632 | solution.py:123
  68.4 2.8 fusion.320
  71.2 3.5 fusion.321
  78.7 5.2 fusion.324
  83.9 3.5 fusion.326
  87.4 3.5 fusion.325
  97.6 2.8 fusion.320
  100.4 3.5 fusion.321
  108.0 5.2 fusion.324
  113.1 3.5 fusion.326
  116.7 3.5 fusion.325
  120.9 4.9 convolution_convert_fusion
  125.9 47.9 %reduce-scatter.3.cloned.1.call-done = bf16[2,384,768]{2,1,0:T(8,128)(2,1)} async-done(((bf16[2,1536,768]{2,1,0:T(8,128)(2,1)}), bf16[2,384,768]{2,1,0:T(8,128)(2,1)}) %reduce-scatter.3.cloned.1.call-update) | async-done | bytes 1179664 | tf_op jit(solution)/shard_map/reduce_scatter | solution.py:126
  177.7 9.2 fusion.165
  186.9 23.4 %multiply_convert_fusion.3 = (bf16[2,384,3072]{2,1,0:T(8,128)(2,1)}, f32[2,384,3072]{2,1,0:T(8,128)}) fusion(f32[2,384,3072]{2,1,0:T(8,128)S(1)} %get-tuple-element.164, f32[3072]{0:T(1024)S(1)} %copy-done.45, u8[384,3072]{1,0:T(8,128)(4,1)S(1)} %get-tuple-element.78, u8[384,3072]{1,0:T(8,128)(4,1)S(1)} %get-tuple-element.77), kind=kLoop, calls=%fused_computation.126 | loop fusion | flops 167510016 | bytes 25964544 | tf_op jit(solution)/shard_map/convert_element_type | solution.py:138
  210.2 12.5 %convert_reduce_fusion = (f32[3072]{0:T(1024)}, bf16[2,384,3072]{2,1,0:T(8,128)(2,1)}) fusion(f32[2,384,3072]{2,1,0:T(8,128)} %get-tuple-element.123, bf16[2,384,768]{2,1,0:T(8,128)(2,1)S(1)} %copy-done.15, bf16[3072,768]{1,0:T(8,128)(2,1)} %param.31, f32[2,384,3072]{2,1,0:T(8,128)S(1)} %get-tuple-element.164, f32[3072]{0:T(1024)S(1)} %copy-done.45), kind=kOutput, calls=%fused_computation.124 | convolution fusion | flops 3663983616 | bytes 29515776 | tf_op jit(solution)/shard_map/rld,fd->rlf/dot_general | solution.py:147
  222.8 8.1 fusion.185
  232.9 2.7 convert_reduce_fusion.4
  235.7 37.6 %all-gather.5.cloned.1.call-done = bf16[2,1536,768]{2,1,0:T(8,128)(2,1)} async-done(((bf16[2,384,768]{2,1,0:T(8,128)(2,1)}), bf16[2,1536,768]{2,1,0:T(8,128)(2,1)}) %all-gather.5.cloned.1.call-update) | async-done | bytes 4718608 | tf_op jit(solution)/shard_map/all_gather | solution.py:160
  273.3 5.0 convolution_convert_fusion.1
  278.3 254.2 %while.23 = (s32[]{:T(128)}, bf16[2,3,1536,192]{2,3,1,0:T(8,128)(2,1)}, bf16[2,3,1536,192]{2,3,1,0:T(8,128)(2,1)}, s32[2,1536]{1,0:T(2,128)S(1)}, f32[2,3,1536]{...) while((s32[]{:T(128)}, ...), condition=%wide.region_19.20_spmd, body=%wide.region_15.19_spmd.sunk | while | flops 4682926080 | bytes 364640672 | solution.py:167
  283.2 2.5 subtract_exponential_fusion.9
  286.7 2.6 copy-done.2
  289.3 2.5 subtract_exponential_fusion.11
  294.2 4.3 copy-done.3
  300.4 5.2 fusion.371
  305.6 15.2 %fusion.377 = bf16[3,64,512]{2,1,0:T(8,128)(2,1)} fusion(bf16[1536,3,64]{0,2,1:T(8,128)(2,1)S(1)} %bitcast.312, f32[3,512,1536]{2,1,0:T(8,128)} %copy-done.4, f32[3,512,1536]{2,1,0:T(8,128)} %fusion.371), kind=kOutput, calls=%fused_computation.94.clone.1 | convolution fusion | flops 320965632 | bytes 19660800 | tf_op jit(solution)/shard_map/while/body/eval_jaxpr/hqk,khe->qhe/dot_general | solution.py:82
  320.8 15.3 %fusion.372 = f32[3,64,1536]{2,1,0:T(8,128)} fusion(bf16[512,3,64]{0,2,1:T(8,128)(2,1)} %bitcast.323, f32[3,512,1536]{2,1,0:T(8,128)} %copy-done.4, f32[3,512,1536]{2,1,0:T(8,128)} %fusion.371), kind=kOutput, calls=%fused_computation.63.clone.1 | convolution fusion | flops 320867328 | bytes 20250624 | tf_op jit(solution)/shard_map/while/body/eval_jaxpr/hqk,qhe->khe/dot_general | solution.py:86
  336.1 5.2 fusion.375
  341.3 14.4 %fusion.379 = bf16[3,64,512]{2,1,0:T(8,128)(2,1)S(1)} fusion(bf16[1536,3,64]{0,2,1:T(8,128)(2,1)S(1)} %bitcast.313, f32[3,512,1536]{2,1,0:T(8,128)} %copy-done.3, f32[3,512,1536]{2,1,0:T(8,128)} %fusion.375), kind=kOutput, calls=%fused_computation.92.clone.1 | convolution fusion | flops 320965632 | bytes 19660800 | tf_op jit(solution)/shard_map/while/body/eval_jaxpr/hqk,khe->qhe/dot_general | solution.py:82
  355.6 5.2 fusion.373
  360.8 15.0 %fusion.378 = bf16[3,64,512]{2,1,0:T(8,128)(2,1)} fusion(bf16[1536,3,64]{0,2,1:T(8,128)(2,1)S(1)} %bitcast.314, f32[3,512,1536]{2,1,0:T(8,128)} %copy-done.2, f32[3,512,1536]{2,1,0:T(8,128)} %fusion.373), kind=kOutput, calls=%fused_computation.93.clone.1 | convolution fusion | flops 320965632 | bytes 19660800 | tf_op jit(solution)/shard_map/while/body/eval_jaxpr/hqk,khe->qhe/dot_general | solution.py:82
  375.8 14.1 %fusion.374 = f32[3,64,1536]{2,1,0:T(8,128)} fusion(bf16[512,3,64]{0,2,1:T(8,128)(2,1)S(1)} %bitcast.321, f32[3,512,1536]{2,1,0:T(8,128)} %copy-done.2, f32[3,512,1536]{2,1,0:T(8,128)} %fusion.373), kind=kOutput, calls=%fused_computation.67.clone.1 | convolution fusion | flops 320867328 | bytes 20250624 | tf_op jit(solution)/shard_map/while/body/eval_jaxpr/hqk,qhe->khe/dot_general | solution.py:86
  389.9 14.1 %fusion.376 = bf16[3,64,1536]{2,1,0:T(8,128)(2,1)S(1)} fusion(f32[3,64,1536]{2,1,0:T(8,128)} %fusion.372, f32[3,64,1536]{2,1,0:T(8,128)} %fusion.374, bf16[512,3,64]{0,2,1:T(8,128)(2,1)S(1)} %bitcast.319, f32[3,512,1536]{2,1,0:T(8,128)} %copy-done.3, f32[3,512,1536]{2,1,0:T(8,128)} %fusion.375), kind=kOutput, calls=%fused_computation.79.clone.1 | convolution fusion | flops 321752064 | bytes 22020096 | tf_op jit(solution)/shard_map/while/body/eval_jaxpr/hqk,qhe->khe/dot_general | solution.py:86
  413.5 2.6 copy-done.2
  421.0 4.3 copy-done.3
  427.2 5.2 fusion.371
  432.4 15.2 %fusion.377 = bf16[3,64,512]{2,1,0:T(8,128)(2,1)} fusion(bf16[1536,3,64]{0,2,1:T(8,128)(2,1)S(1)} %bitcast.312, f32[3,512,1536]{2,1,0:T(8,128)} %copy-done.4, f32[3,512,1536]{2,1,0:T(8,128)} %fusion.371), kind=kOutput, calls=%fused_computation.94.clone.1 | convolution fusion | flops 320965632 | bytes 19660800 | tf_op jit(solution)/shard_map/while/body/eval_jaxpr/hqk,khe->qhe/dot_general | solution.py:82
  447.6 15.3 %fusion.372 = f32[3,64,1536]{2,1,0:T(8,128)} fusion(bf16[512,3,64]{0,2,1:T(8,128)(2,1)} %bitcast.323, f32[3,512,1536]{2,1,0:T(8,128)} %copy-done.4, f32[3,512,1536]{2,1,0:T(8,128)} %fusion.371), kind=kOutput, calls=%fused_computation.63.clone.1 | convolution fusion | flops 320867328 | bytes 20250624 | tf_op jit(solution)/shard_map/while/body/eval_jaxpr/hqk,qhe->khe/dot_general | solution.py:86
  462.9 5.2 fusion.375
  468.1 14.4 %fusion.379 = bf16[3,64,512]{2,1,0:T(8,128)(2,1)S(1)} fusion(bf16[1536,3,64]{0,2,1:T(8,128)(2,1)S(1)} %bitcast.313, f32[3,512,1536]{2,1,0:T(8,128)} %copy-done.3, f32[3,512,1536]{2,1,0:T(8,128)} %fusion.375), kind=kOutput, calls=%fused_computation.92.clone.1 | convolution fusion | flops 320965632 | bytes 19660800 | tf_op jit(solution)/shard_map/while/body/eval_jaxpr/hqk,khe->qhe/dot_general | solution.py:82
  482.5 5.2 fusion.373
  487.6 15.0 %fusion.378 = bf16[3,64,512]{2,1,0:T(8,128)(2,1)} fusion(bf16[1536,3,64]{0,2,1:T(8,128)(2,1)S(1)} %bitcast.314, f32[3,512,1536]{2,1,0:T(8,128)} %copy-done.2, f32[3,512,1536]{2,1,0:T(8,128)} %fusion.373), kind=kOutput, calls=%fused_computation.93.clone.1 | convolution fusion | flops 320965632 | bytes 19660800 | tf_op jit(solution)/shard_map/while/body/eval_jaxpr/hqk,khe->qhe/dot_general | solution.py:82
  502.6 14.1 %fusion.374 = f32[3,64,1536]{2,1,0:T(8,128)} fusion(bf16[512,3,64]{0,2,1:T(8,128)(2,1)S(1)} %bitcast.321, f32[3,512,1536]{2,1,0:T(8,128)} %copy-done.2, f32[3,512,1536]{2,1,0:T(8,128)} %fusion.373), kind=kOutput, calls=%fused_computation.67.clone.1 | convolution fusion | flops 320867328 | bytes 20250624 | tf_op jit(solution)/shard_map/while/body/eval_jaxpr/hqk,qhe->khe/dot_general | solution.py:86
  516.8 14.1 %fusion.376 = bf16[3,64,1536]{2,1,0:T(8,128)(2,1)S(1)} fusion(f32[3,64,1536]{2,1,0:T(8,128)} %fusion.372, f32[3,64,1536]{2,1,0:T(8,128)} %fusion.374, bf16[512,3,64]{0,2,1:T(8,128)(2,1)S(1)} %bitcast.319, f32[3,512,1536]{2,1,0:T(8,128)} %copy-done.3, f32[3,512,1536]{2,1,0:T(8,128)} %fusion.375), kind=kOutput, calls=%fused_computation.79.clone.1 | convolution fusion | flops 321752064 | bytes 22020096 | tf_op jit(solution)/shard_map/while/body/eval_jaxpr/hqk,qhe->khe/dot_general | solution.py:86
  532.5 4.6 fusion.177
  537.2 6.2 fusion.174
  543.4 7.7 bitcast_convert_fusion
  551.2 10.5 %convolution_bitcast_fusion = f32[3072,768]{1,0:T(8,128)} fusion(bf16[2,384,3072]{2,1,0:T(8,128)(2,1)} %get-tuple-element.122, bf16[2,384,768]{2,1,0:T(8,128)(2,1)} %param.33), kind=kOutput, calls=%fused_computation.140 | convolution fusion | flops 3623878656 | bytes 15335424 | tf_op jit(solution)/shard_map/rlf,rld->fd/dot_general | solution.py:143
  561.7 9.2 convolution_bitcast_fusion.1
  571.7 8.8 add_convert_fusion.3
  580.9 21.5 %psum.87 = bf16[2,192]{1,0:T(2,128)(2,1)S(1)} all-reduce(bf16[2,192]{1,0:T(2,128)(2,1)S(1)} %slice_reduce_fusion), channel_id=1, replica_groups=mesh['dp'=8,'th'=2,'tw'=2] {'dp'}, use_global_device_ids=true, to_apply=%region_29.30 | all-reduce | flops 384 | bytes 1536 | tf_op jit(solution)/shard_map/psum | solution.py:178
  603.0 20.8 %all-reduce.8.cloned.1.call-done = (bf16[3,768,192]{1,2,0:T(8,128)(2,1)}, bf16[192,768]{1,0:T(8,128)(2,1)}) async-done(((bf16[3,768,192]{1,2,0:T(8,128)(2,1)}, bf16[192,768]{1,0:T(8,128)(2,1)}), (bf16[3,768,192]{1,2,0:T(8,128)(2,1)}, bf16[192,768]{1,0:T(8,128)(2,1)})) %all-reduce.8.cloned.1.call-update) | async-done | bytes 1179664 | tf_op jit(solution)/shard_map/psum | solution.py:177
  625.6 2.5 convert_element_type.154
  628.1 45.2 %reduce-scatter.5.cloned.1.call-done = bf16[2,384,768]{2,1,0:T(8,128)(2,1)} async-done(((bf16[2,1536,768]{2,1,0:T(8,128)(2,1)}), bf16[2,384,768]{2,1,0:T(8,128)(2,1)}) %reduce-scatter.5.cloned.1.call-update) | async-done | bytes 1179664 | tf_op jit(solution)/shard_map/reduce_scatter | solution.py:171
  675.6 2.7 fusion.163
  678.4 3.0 convert_reduce_fusion.3
  681.4 42.5 %all-reduce = (f32[768]{0:T(1024)}, f32[768]{0:T(1024)}, f32[768]{0:T(1024)}, f32[768]{0:T(1024)}, f32[768]{0:T(1024)}, /*index=5*/f32[3072]{0:T(1024)}, f32[768]{0:T(1024)}) all-reduce(f32[768]{0:T(1024)S(1)} %get-tuple-element.81, f32[768]{0:T(1024)S(1)} %get-tuple-element.85, ...), channel_id=1, replica_groups=mesh['dp'=8,'th'=2,'tw'=2] {'dp','th','tw'}, use_global_device_ids=true, to_apply=%region_24.25 | all-reduce | flops 7680 | bytes 61440 | tf_op jit(solution)/shard_map/psum | solution.py:181
  724.0 262.5 %all-reduce.6.cloned.1.call-done = (f32[768,3072]{1,0:T(8,128)}, f32[3072,768]{1,0:T(8,128)}) async-done(((f32[768,3072]{1,0:T(8,128)}, f32[3072,768]{1,0:T(8,128)}), (f32[768,3072]{1,0:T(8,128)}, f32[3072,768]{1,0:T(8,128)})) %all-reduce.6.cloned.1.call-update) | async-done | bytes 18874384 | tf_op jit(solution)/shard_map/psum | solution.py:181
  986.5 8.8 copy.59
  995.2 3.7 copy.60
  (212 shorter events, 65.0 us)
Async XLA Ops:
  7.2 47.7 %copy-start = (bf16[3,768,192]{1,2,0:T(8,128)(2,1)S(1)}, bf16[3,768,192]{1,2,0:T(8,128)(2,1)}, u32[]{:S(2)}) copy-start(bf16[3,768,192]{1,2,0:T(8,128)(2,1)} %param.23) | copy-start | bytes 2654212
  7.2 7.5 copy-start.48
  7.2 47.7 %all-gather.3.cloned.1.call-start = ((), (), s32[]{:S(2)}) async-start(), calls=%async_computation.2 | async-start | bytes 5898240 | tf_op jit(solution)/shard_map/all_gather | solution.py:119
  8.8 2.3 copy-start.32
  14.6 159.3 %reduce-scatter.3.cloned.1.call-start = ((), (), s32[]{:S(2)}) async-start(), calls=%async_computation.3 | async-start | bytes 5898240 | tf_op jit(solution)/shard_map/reduce_scatter | solution.py:126
  14.8 46.8 %copy-start.20 = (s32[2,1536]{1,0:T(2,128)S(1)}, s32[2,1536]{1,0:T(2,128)}, u32[]{:S(2)}) copy-start(s32[2,1536]{1,0:T(2,128)} %param.20) | copy-start | bytes 36868
  120.8 5.0 copy-start.17
  120.9 53.0 %copy-start.5 = (bf16[2,384,768]{2,1,0:T(8,128)(2,1)S(1)}, bf16[2,384,768]{2,1,0:T(8,128)(2,1)}, u32[]{:S(2)}) copy-start(bf16[2,384,768]{2,1,0:T(8,128)(2,1)} %param.19) | copy-start | bytes 3538948
  120.9 53.0 %copy-start.21 = (f32[768]{0:T(1024)S(1)}, f32[768]{0:T(1024)}, u32[]{:S(2)}) copy-start(f32[768]{0:T(1024)} %param.26) | copy-start | bytes 9220
  125.8 51.8 %copy-start.25 = (f32[768]{0:T(1024)S(1)}, f32[768]{0:T(1024)}, u32[]{:S(2)}) copy-start(f32[768]{0:T(1024)} %param.27) | copy-start | bytes 9220
  125.8 51.8 %copy-start.30 = (f32[768]{0:T(1024)S(1)}, f32[768]{0:T(1024)}, u32[]{:S(2)}) copy-start(f32[768]{0:T(1024)} %param.28) | copy-start | bytes 9220
  125.8 51.8 %copy-start.45 = (f32[3072]{0:T(1024)S(1)}, f32[3072]{0:T(1024)}, u32[]{:S(2)}) copy-start(f32[3072]{0:T(1024)} %param.30) | copy-start | bytes 36868
  125.8 147.5 %all-gather.5.cloned.1.call-start = ((), (), s32[]{:S(2)}) async-start(), calls=%async_computation.4 | async-start | bytes 5898240 | tf_op jit(solution)/shard_map/all_gather | solution.py:160
  173.8 3.8 copy-start.7
  175.7 57.2 %copy-start.23 = (f32[2,384]{1,0:T(2,128)}, f32[2,384]{1,0:T(2,128)S(1)}, u32[]{:S(2)}) copy-start(f32[2,384]{1,0:T(2,128)S(1)} %broadcast_multiply_fusion) | copy-start | bytes 9220
  177.7 55.3 %copy-start.27 = (f32[2,384]{1,0:T(2,128)}, f32[2,384]{1,0:T(2,128)S(1)}, u32[]{:S(2)}) copy-start(f32[2,384]{1,0:T(2,128)S(1)} %fusion.183) | copy-start | bytes 9220
  186.8 23.4 %copy-start.15 = (bf16[2,384,768]{2,1,0:T(8,128)(2,1)S(1)}, bf16[2,384,768]{2,1,0:T(8,128)(2,1)}, u32[]{:S(2)}) copy-start(bf16[2,384,768]{2,1,0:T(8,128)(2,1)} %param.33) | copy-start | bytes 3538948
  230.9 4.8 copy-start.9
  230.9 4.8 copy-start.35
  232.9 40.4 %copy-start.29 = (bf16[192,768]{1,0:T(8,128)(2,1)S(1)}, bf16[192,768]{1,0:T(8,128)(2,1)}, u32[]{:S(2)}) copy-start(bf16[192,768]{1,0:T(8,128)(2,1)} %param.25) | copy-start | bytes 884740
  232.9 45.4 %copy-start.39 = (f32[2,384]{1,0:T(2,128)}, f32[2,384]{1,0:T(2,128)S(1)}, u32[]{:S(2)}) copy-start(f32[2,384]{1,0:T(2,128)S(1)} %negate_multiply_fusion.2) | copy-start | bytes 9220
  235.7 388.1 %all-reduce.8.cloned.1.call-start = ((), (), s32[]{:S(2)}) async-start(), calls=%async_computation.7 | async-start | bytes 2359296 | tf_op jit(solution)/shard_map/psum | solution.py:177
  278.7 2.8 copy-start.1
  281.7 4.9 copy-start.12
  285.6 3.6 copy-start.2
  291.7 7.7 copy-start.4
  294.2 4.3 copy-start.3
  389.9 14.2 %copy-start.13 = (bf16[3,64,512]{2,1,0:T(8,128)(2,1)S(1)}, bf16[3,64,512]{2,1,0:T(8,128)(2,1)}, u32[]{:S(2)}) copy-start(bf16[3,64,512]{2,1,0:T(8,128)(2,1)} %fusion.377) | copy-start | bytes 589828 | tf_op jit(solution)/shard_map/while
  389.9 14.2 %copy-start.14 = (bf16[3,64,512]{2,1,0:T(8,128)(2,1)S(1)}, bf16[3,64,512]{2,1,0:T(8,128)(2,1)}, u32[]{:S(2)}) copy-start(bf16[3,64,512]{2,1,0:T(8,128)(2,1)} %fusion.378) | copy-start | bytes 589828 | tf_op jit(solution)/shard_map/while
  405.6 2.8 copy-start.1
  408.6 4.9 copy-start.12
  412.5 3.6 copy-start.2
  418.6 7.7 copy-start.4
  421.0 4.3 copy-start.3
  516.7 14.2 %copy-start.13 = (bf16[3,64,512]{2,1,0:T(8,128)(2,1)S(1)}, bf16[3,64,512]{2,1,0:T(8,128)(2,1)}, u32[]{:S(2)}) copy-start(bf16[3,64,512]{2,1,0:T(8,128)(2,1)} %fusion.377) | copy-start | bytes 589828 | tf_op jit(solution)/shard_map/while
  516.8 14.2 %copy-start.14 = (bf16[3,64,512]{2,1,0:T(8,128)(2,1)S(1)}, bf16[3,64,512]{2,1,0:T(8,128)(2,1)}, u32[]{:S(2)}) copy-start(bf16[3,64,512]{2,1,0:T(8,128)(2,1)} %fusion.378) | copy-start | bytes 589828 | tf_op jit(solution)/shard_map/while
  532.5 4.7 copy-start.18
  543.3 130.0 %reduce-scatter.5.cloned.1.call-start = ((), (), s32[]{:S(2)}) async-start(), calls=%async_computation.5 | async-start | bytes 5898240 | tf_op jit(solution)/shard_map/reduce_scatter | solution.py:171
  551.1 435.4 %all-reduce.6.cloned.1.call-start = ((), (), s32[]{:S(2)}) async-start(), calls=%async_computation.6 | async-start | bytes 37748736 | tf_op jit(solution)/shard_map/psum | solution.py:181
  551.1 10.6 %copy-start.6 = (bf16[2,384,768]{2,1,0:T(8,128)(2,1)S(1)}, bf16[2,384,768]{2,1,0:T(8,128)(2,1)}, u32[]{:S(2)}) copy-start(bf16[2,384,768]{2,1,0:T(8,128)(2,1)} %param.19) | copy-start | bytes 3538948
  551.1 10.6 %copy-start.8 = (bf16[2,384,768]{2,1,0:T(8,128)(2,1)S(1)}, bf16[2,384,768]{2,1,0:T(8,128)(2,1)}, u32[]{:S(2)}) copy-start(bf16[2,384,768]{2,1,0:T(8,128)(2,1)} %reduce-scatter.3.cloned.1.call-done) | copy-start | bytes 3538948
  551.2 10.5 %copy-start.22 = (f32[768]{0:T(1024)S(1)}, f32[768]{0:T(1024)}, u32[]{:S(2)}) copy-start(f32[768]{0:T(1024)} %param.26) | copy-start | bytes 9220
  551.2 10.5 %copy-start.24 = (f32[2,384]{1,0:T(2,128)S(1)}, f32[2,384]{1,0:T(2,128)}, u32[]{:S(2)}) copy-start(f32[2,384]{1,0:T(2,128)} %copy-done.23) | copy-start | bytes 9220
  551.2 10.5 %copy-start.26 = (f32[768]{0:T(1024)S(1)}, f32[768]{0:T(1024)}, u32[]{:S(2)}) copy-start(f32[768]{0:T(1024)} %param.27) | copy-start | bytes 9220
  551.2 10.5 %copy-start.28 = (f32[2,384]{1,0:T(2,128)S(1)}, f32[2,384]{1,0:T(2,128)}, u32[]{:S(2)}) copy-start(f32[2,384]{1,0:T(2,128)} %copy-done.27) | copy-start | bytes 9220
  551.2 10.5 %copy-start.31 = (f32[768]{0:T(1024)S(1)}, f32[768]{0:T(1024)}, u32[]{:S(2)}) copy-start(f32[768]{0:T(1024)} %param.28) | copy-start | bytes 9220
  571.0 0.7 copy-start.49
  571.7 8.8 copy-start.19
  580.5 92.9 %copy-start.33 = (f32[2,384]{1,0:T(2,128)S(1)}, f32[2,384]{1,0:T(2,128)}, u32[]{:S(2)}) copy-start(f32[2,384]{1,0:T(2,128)} %copy-done.32) | copy-start | bytes 9220
  580.5 92.9 %copy-start.34 = (f32[768]{0:T(1024)S(1)}, f32[768]{0:T(1024)}, u32[]{:S(2)}) copy-start(f32[768]{0:T(1024)} %param.21) | copy-start | bytes 9220
  580.5 95.1 %copy-start.42 = (f32[2,384]{1,0:T(2,128)S(1)}, f32[2,384]{1,0:T(2,128)}, u32[]{:S(2)}) copy-start(f32[2,384]{1,0:T(2,128)} %copy-done.41) | copy-start | bytes 9220
  580.5 95.1 %copy-start.38 = (f32[2,384]{1,0:T(2,128)S(1)}, f32[2,384]{1,0:T(2,128)}, u32[]{:S(2)}) copy-start(f32[2,384]{1,0:T(2,128)} %copy-done.37) | copy-start | bytes 9220
  580.9 97.5 %copy-start.36 = (f32[2,384]{1,0:T(2,128)S(1)}, f32[2,384]{1,0:T(2,128)}, u32[]{:S(2)}) copy-start(f32[2,384]{1,0:T(2,128)} %copy-done.35) | copy-start | bytes 9220
  580.9 97.5 %copy-start.40 = (f32[2,384]{1,0:T(2,128)S(1)}, f32[2,384]{1,0:T(2,128)}, u32[]{:S(2)}) copy-start(f32[2,384]{1,0:T(2,128)} %copy-done.39) | copy-start | bytes 9220
  673.3 5.1 copy-start.10
  673.3 5.1 copy-start.11
  673.3 5.1 copy-start.16
  678.3 3.1 copy-start.43
  678.3 3.1 copy-start.44
  678.3 3.1 copy-start.46
  678.4 3.1 copy-start.47
  986.5 8.8 slice-start
  986.5 8.8 slice-start.1
  986.5 8.8 slice-start.2
  (2 other events, 1.2 us)
Sparse Core Ops, SparseCore 0:
  14.7 40.1 all-gather.2
  126.0 47.8 reduce-scatter.2
  235.8 37.4 all-gather.4
  543.5 80.2 all-reduce.7
  626.2 47.1 reduce-scatter.4
  681.3 305.1 all-reduce.5
where the time goes:
time: 1010 us
  waiting for transfers between devices  454 us (45%)
  matrix products  354 us (35%)
  other arithmetic  75.9 us (8%)
  blocking collectives  64 us (6%)
  local copies, waits for them, and re-layouts  40.5 us (4%)
  between operations  14.8 us (1%)
    psum x1, waiting for transfers between devices, body(): lax.psum((grad_gain_one, grad_shift_one, grad_b_out, grad_gain_two, grad_...  263 us
    dot_general x6, matrix products, row_backward(): jnp.einsum('hqk,khe->qhe', score_grad, key_rows, preferred_element_type=j...  89.1 us
    dot_general x6, matrix products, row_backward(): jnp.einsum('hqk,qhe->khe', score_grad, query_block, preferred_element_typ...  87.3 us
    reduce_scatter x1, waiting for transfers between devices, body(): lax.psum_scatter(partial_out.astype(jnp.bfloat16), ('th', 'tw'), scatter_...  47.9 us
    reduce_scatter x1, waiting for transfers between devices, body(): lax.psum_scatter(grad_normed.astype(jnp.bfloat16), ('th', 'tw'), scatter_...  45.2 us
    psum x1, blocking collectives, body(): lax.psum((grad_gain_one, grad_shift_one, grad_b_out, grad_gain_two, grad_...  42.5 us
    all_gather x1, waiting for transfers between devices, body(): gathered = lax.all_gather(normed_low, ('th', 'tw'), axis=1, tiled=True)  40.1 us
    all_gather x1, waiting for transfers between devices, body(): grad_whole = lax.all_gather(grad_branch, ('th', 'tw'), axis=1, tiled=True)  37.6 us
  transfers between devices with their start and end apart: 6, of which 6 were waited for; matrix products, arithmetic and copies ran while one was open for 5% of the time, Pallas kernels for 0%

commit v1 on v0

--- a/solution.py
+++ b/solution.py
@@ -116,7 +116,19 @@
     inputs = tokens.astype(jnp.float32)
     normed_one, norm_one_back = jax.vjp(layer_norm, inputs, norm1_gain, norm1_shift)
     normed_low = normed_one.astype(jnp.bfloat16)
-    gathered = lax.all_gather(normed_low, ("th", "tw"), axis=1, tiled=True)
+    ways, here, step = (
+        lax.axis_size(("th", "tw")),
+        lax.axis_index(("th", "tw")),
+        normed_low.shape[1],
+    )
+    line, have = (normed_low, 1)
+    while have < ways:
+        line = jnp.concatenate(
+            [line, lax.ppermute(line, ("th", "tw"), [(d, (d - have) % ways) for d in range(ways)])],
+            axis=1,
+        )
+        have = 2 * have
+    gathered = jnp.roll(line, here * step, axis=1)
     bias_rows = jnp.stack([b_qv[0], jnp.zeros_like(b_qv[0]), b_qv[1]])
     projected = jnp.einsum("rld,cde->rcle", gathered, w_qkv, preferred_element_type=jnp.float32)
     projected_low = (projected + bias_rows[None, :, None, :]).astype(jnp.bfloat16)

time: 1010 us -> 1010 us (level)
    all_gather x1 -> x0, waiting for transfers between devices: 40.1 us -> none  [body(): gathered = lax.all_gather(normed_low, ('th', 'tw'), axis=1, tiled=True)]
    ppermute x0 -> x2, waiting for transfers between devices: none -> 30.1 us  [body(): lax.ppermute(line, ('th', 'tw'), [(d, (d - have) % ways) for d in range(w...]
    unnamed x94 -> x102, local copies, waits for them, and re-layouts: 14.5 us -> 20.4 us
  transfers between devices with their start and end apart: 6 -> 7, of which waited for: 6 -> 7; matrix products, arithmetic and copies ran while one was open for 5% -> 5% of each run, Pallas kernels for 0% -> 0%
where the time goes in v1:
time: 1010 us
  waiting for transfers between devices  446 us (44%)
  matrix products  352 us (35%)
  other arithmetic  77.6 us (8%)
  blocking collectives  64 us (6%)
  local copies, waits for them, and re-layouts  49.7 us (5%)
  between operations  14.5 us (1%)
    psum x1, waiting for transfers between devices, body(): lax.psum((grad_gain_one, grad_shift_one, grad_b_out, grad_gain_two, grad_...  263 us
    dot_general x6, matrix products, row_backward(): jnp.einsum('hqk,khe->qhe', score_grad, key_rows, preferred_element_type=j...  88.3 us
    dot_general x6, matrix products, row_backward(): jnp.einsum('hqk,qhe->khe', score_grad, query_block, preferred_element_typ...  86.7 us
    reduce_scatter x1, waiting for transfers between devices, body(): lax.psum_scatter(partial_out.astype(jnp.bfloat16), ('th', 'tw'), scatter_...  50 us
    reduce_scatter x1, waiting for transfers between devices, body(): lax.psum_scatter(grad_normed.astype(jnp.bfloat16), ('th', 'tw'), scatter_...  45.2 us
    psum x1, blocking collectives, body(): lax.psum((grad_gain_one, grad_shift_one, grad_b_out, grad_gain_two, grad_...  42.5 us
    all_gather x1, waiting for transfers between devices, body(): grad_whole = lax.all_gather(grad_branch, ('th', 'tw'), axis=1, tiled=True)  37.6 us
    dot_general x6, matrix products, row_backward(): jnp.einsum('qhe,khe->hqk', upstream, value_rows, preferred_element_type=j...  30.9 us
  transfers between devices with their start and end apart: 7, of which 7 were waited for; matrix products, arithmetic and copies ran while one was open for 5% of the time, Pallas kernels for 0%

profile of v1, /device:TPU:0, one launch (start us, length us, event | category | flops | bytes accessed | tf_op | source)
XLA Modules:
  0.0 1008.1 jit_solution(17914892453834384539)
XLA Ops:
  11.2 2.8 constant_dynamic-update-slice_fusion.5
  16.4 26.5 %collective-permute-done = bf16[2,384,768]{2,1,0:T(8,128)(2,1)S(1)} collective-permute-done((bf16[2,384,768]{2,1,0:T(8,128)(2,1)S(1)}, bf16[2,384,768]{2,1,0:T(8,128)(2,1)S(1)}, u32[]{:S(2)}, u32[]{:S(2)}) %collective-permute-start) | collective-permute-done | bytes 1179680 | tf_op jit(solution)/shard_map/ppermute | solution.py:127
  45.7 3.6 collective-permute-done.1
  49.4 3.2 constant_dynamic-update-slice_fusion.3
  54.8 3.2 constant_dynamic-update-slice_fusion
  58.0 6.9 fusion.156
  64.9 59.3 %while.22 = (s32[]{:T(128)}, bf16[2,1536,192]{1,2,0:T(8,128)(2,1)S(1)}, f32[2,3,1536]{2,1,0:T(4,128)S(1)}, bf16[2,3,1536,192]{2,3,1,0:T(8,128)(2,1)}, s32[2,1536...) while((s32[]{:T(128)}, bf16[2,1536,192]{1,2,0:T(8,128)(2,1)S(1)}, ...), condition=%wide.region_9.10_spmd, body=%wide.region_2.9_spmd.sunk | while | flops 1901302272 | bytes 107581632 | solution.py:135
  71.7 2.8 fusion.325
  74.5 3.5 fusion.326
  82.0 5.2 fusion.329
  87.2 3.5 fusion.331
  90.7 3.5 fusion.330
  100.9 2.8 fusion.325
  103.7 3.5 fusion.326
  111.3 5.2 fusion.329
  116.4 3.5 fusion.331
  120.0 3.5 fusion.330
  124.2 4.9 convolution_convert_fusion
  129.2 50.0 %reduce-scatter.3.cloned.1.call-done = bf16[2,384,768]{2,1,0:T(8,128)(2,1)} async-done(((bf16[2,1536,768]{2,1,0:T(8,128)(2,1)}), bf16[2,384,768]{2,1,0:T(8,128)(2,1)}) %reduce-scatter.3.cloned.1.call-update) | async-done | bytes 1179664 | tf_op jit(solution)/shard_map/reduce_scatter | solution.py:138
  183.0 9.2 fusion.167
  192.2 23.5 %multiply_convert_fusion.3 = (bf16[2,384,3072]{2,1,0:T(8,128)(2,1)}, f32[2,384,3072]{2,1,0:T(8,128)}) fusion(f32[2,384,3072]{2,1,0:T(8,128)S(1)} %get-tuple-element.166, f32[3072]{0:T(1024)S(1)} %copy-done.46, u8[384,3072]{1,0:T(8,128)(4,1)S(1)} %get-tuple-element.78, u8[384,3072]{1,0:T(8,128)(4,1)S(1)} %get-tuple-element.77), kind=kLoop, calls=%fused_computation.126 | loop fusion | flops 167510016 | bytes 25964544 | tf_op jit(solution)/shard_map/convert_element_type | solution.py:150
  215.7 12.5 %convert_reduce_fusion = (f32[3072]{0:T(1024)}, bf16[2,384,3072]{2,1,0:T(8,128)(2,1)}) fusion(f32[2,384,3072]{2,1,0:T(8,128)} %get-tuple-element.123, bf16[2,384,768]{2,1,0:T(8,128)(2,1)S(1)} %copy-done.15, bf16[3072,768]{1,0:T(8,128)(2,1)} %param.31, f32[2,384,3072]{2,1,0:T(8,128)S(1)} %get-tuple-element.166, f32[3072]{0:T(1024)S(1)} %copy-done.46), kind=kOutput, calls=%fused_computation.124 | convolution fusion | flops 3663983616 | bytes 29515776 | tf_op jit(solution)/shard_map/rld,fd->rlf/dot_general | solution.py:159
  228.2 8.1 fusion.189
  238.3 2.7 convert_reduce_fusion.4
  241.1 37.6 %all-gather.2.cloned.1.call-done = bf16[2,1536,768]{2,1,0:T(8,128)(2,1)} async-done(((bf16[2,384,768]{2,1,0:T(8,128)(2,1)}), bf16[2,1536,768]{2,1,0:T(8,128)(2,1)}) %all-gather.2.cloned.1.call-update) | async-done | bytes 4718608 | tf_op jit(solution)/shard_map/all_gather | solution.py:172
  278.7 5.0 convolution_convert_fusion.1
  283.7 252.7 %while.23 = (s32[]{:T(128)}, bf16[2,3,1536,192]{2,3,1,0:T(8,128)(2,1)}, bf16[2,3,1536,192]{2,3,1,0:T(8,128)(2,1)}, s32[2,1536]{1,0:T(2,128)S(1)}, f32[2,3,1536]{...) while((s32[]{:T(128)}, ...), condition=%wide.region_19.20_spmd, body=%wide.region_15.19_spmd.sunk | while | flops 4682926080 | bytes 364640672 | solution.py:179
  292.0 2.6 copy-done.2
  299.6 4.3 copy-done.3
  305.8 5.1 fusion.376
  310.9 15.2 %fusion.382 = bf16[3,64,512]{2,1,0:T(8,128)(2,1)} fusion(bf16[1536,3,64]{0,2,1:T(8,128)(2,1)S(1)} %bitcast.312, f32[3,512,1536]{2,1,0:T(8,128)} %copy-done.4, f32[3,512,1536]{2,1,0:T(8,128)} %fusion.376), kind=kOutput, calls=%fused_computation.94.clone.1 | convolution fusion | flops 320965632 | bytes 19660800 | tf_op jit(solution)/shard_map/while/body/eval_jaxpr/hqk,khe->qhe/dot_general | solution.py:82
  326.1 15.3 %fusion.377 = f32[3,64,1536]{2,1,0:T(8,128)} fusion(bf16[512,3,64]{0,2,1:T(8,128)(2,1)} %bitcast.323, f32[3,512,1536]{2,1,0:T(8,128)} %copy-done.4, f32[3,512,1536]{2,1,0:T(8,128)} %fusion.376), kind=kOutput, calls=%fused_computation.63.clone.1 | convolution fusion | flops 320867328 | bytes 20250624 | tf_op jit(solution)/shard_map/while/body/eval_jaxpr/hqk,qhe->khe/dot_general | solution.py:86
  341.5 5.1 fusion.380
  346.6 14.2 %fusion.384 = bf16[3,64,512]{2,1,0:T(8,128)(2,1)S(1)} fusion(bf16[1536,3,64]{0,2,1:T(8,128)(2,1)S(1)} %bitcast.313, f32[3,512,1536]{2,1,0:T(8,128)} %copy-done.3, f32[3,512,1536]{2,1,0:T(8,128)} %fusion.380), kind=kOutput, calls=%fused_computation.92.clone.1 | convolution fusion | flops 320965632 | bytes 19660800 | tf_op jit(solution)/shard_map/while/body/eval_jaxpr/hqk,khe->qhe/dot_general | solution.py:82
  360.8 5.2 fusion.378
  366.0 14.8 %fusion.383 = bf16[3,64,512]{2,1,0:T(8,128)(2,1)} fusion(bf16[1536,3,64]{0,2,1:T(8,128)(2,1)S(1)} %bitcast.314, f32[3,512,1536]{2,1,0:T(8,128)} %copy-done.2, f32[3,512,1536]{2,1,0:T(8,128)} %fusion.378), kind=kOutput, calls=%fused_computation.93.clone.1 | convolution fusion | flops 320965632 | bytes 19660800 | tf_op jit(solution)/shard_map/while/body/eval_jaxpr/hqk,khe->qhe/dot_general | solution.py:82
  380.8 14.1 %fusion.379 = f32[3,64,1536]{2,1,0:T(8,128)} fusion(bf16[512,3,64]{0,2,1:T(8,128)(2,1)S(1)} %bitcast.321, f32[3,512,1536]{2,1,0:T(8,128)} %copy-done.2, f32[3,512,1536]{2,1,0:T(8,128)} %fusion.378), kind=kOutput, calls=%fused_computation.67.clone.1 | convolution fusion | flops 320867328 | bytes 20250624 | tf_op jit(solution)/shard_map/while/body/eval_jaxpr/hqk,qhe->khe/dot_general | solution.py:86
  394.8 13.9 %fusion.381 = bf16[3,64,1536]{2,1,0:T(8,128)(2,1)S(1)} fusion(f32[3,64,1536]{2,1,0:T(8,128)} %fusion.377, f32[3,64,1536]{2,1,0:T(8,128)} %fusion.379, bf16[512,3,64]{0,2,1:T(8,128)(2,1)S(1)} %bitcast.319, f32[3,512,1536]{2,1,0:T(8,128)} %copy-done.3, f32[3,512,1536]{2,1,0:T(8,128)} %fusion.380), kind=kOutput, calls=%fused_computation.79.clone.1 | convolution fusion | flops 321752064 | bytes 22020096 | tf_op jit(solution)/shard_map/while/body/eval_jaxpr/hqk,qhe->khe/dot_general | solution.py:86
  418.1 2.6 copy-done.2
  425.7 4.3 copy-done.3
  431.9 5.1 fusion.376
  437.0 15.2 %fusion.382 = bf16[3,64,512]{2,1,0:T(8,128)(2,1)} fusion(bf16[1536,3,64]{0,2,1:T(8,128)(2,1)S(1)} %bitcast.312, f32[3,512,1536]{2,1,0:T(8,128)} %copy-done.4, f32[3,512,1536]{2,1,0:T(8,128)} %fusion.376), kind=kOutput, calls=%fused_computation.94.clone.1 | convolution fusion | flops 320965632 | bytes 19660800 | tf_op jit(solution)/shard_map/while/body/eval_jaxpr/hqk,khe->qhe/dot_general | solution.py:82
  452.2 15.3 %fusion.377 = f32[3,64,1536]{2,1,0:T(8,128)} fusion(bf16[512,3,64]{0,2,1:T(8,128)(2,1)} %bitcast.323, f32[3,512,1536]{2,1,0:T(8,128)} %copy-done.4, f32[3,512,1536]{2,1,0:T(8,128)} %fusion.376), kind=kOutput, calls=%fused_computation.63.clone.1 | convolution fusion | flops 320867328 | bytes 20250624 | tf_op jit(solution)/shard_map/while/body/eval_jaxpr/hqk,qhe->khe/dot_general | solution.py:86
  467.6 5.1 fusion.380
  472.7 14.2 %fusion.384 = bf16[3,64,512]{2,1,0:T(8,128)(2,1)S(1)} fusion(bf16[1536,3,64]{0,2,1:T(8,128)(2,1)S(1)} %bitcast.313, f32[3,512,1536]{2,1,0:T(8,128)} %copy-done.3, f32[3,512,1536]{2,1,0:T(8,128)} %fusion.380), kind=kOutput, calls=%fused_computation.92.clone.1 | convolution fusion | flops 320965632 | bytes 19660800 | tf_op jit(solution)/shard_map/while/body/eval_jaxpr/hqk,khe->qhe/dot_general | solution.py:82
  486.9 5.2 fusion.378
  492.1 14.8 %fusion.383 = bf16[3,64,512]{2,1,0:T(8,128)(2,1)} fusion(bf16[1536,3,64]{0,2,1:T(8,128)(2,1)S(1)} %bitcast.314, f32[3,512,1536]{2,1,0:T(8,128)} %copy-done.2, f32[3,512,1536]{2,1,0:T(8,128)} %fusion.378), kind=kOutput, calls=%fused_computation.93.clone.1 | convolution fusion | flops 320965632 | bytes 19660800 | tf_op jit(solution)/shard_map/while/body/eval_jaxpr/hqk,khe->qhe/dot_general | solution.py:82
  506.9 14.1 %fusion.379 = f32[3,64,1536]{2,1,0:T(8,128)} fusion(bf16[512,3,64]{0,2,1:T(8,128)(2,1)S(1)} %bitcast.321, f32[3,512,1536]{2,1,0:T(8,128)} %copy-done.2, f32[3,512,1536]{2,1,0:T(8,128)} %fusion.378), kind=kOutput, calls=%fused_computation.67.clone.1 | convolution fusion | flops 320867328 | bytes 20250624 | tf_op jit(solution)/shard_map/while/body/eval_jaxpr/hqk,qhe->khe/dot_general | solution.py:86
  520.9 13.9 %fusion.381 = bf16[3,64,1536]{2,1,0:T(8,128)(2,1)S(1)} fusion(f32[3,64,1536]{2,1,0:T(8,128)} %fusion.377, f32[3,64,1536]{2,1,0:T(8,128)} %fusion.379, bf16[512,3,64]{0,2,1:T(8,128)(2,1)S(1)} %bitcast.319, f32[3,512,1536]{2,1,0:T(8,128)} %copy-done.3, f32[3,512,1536]{2,1,0:T(8,128)} %fusion.380), kind=kOutput, calls=%fused_computation.79.clone.1 | convolution fusion | flops 321752064 | bytes 22020096 | tf_op jit(solution)/shard_map/while/body/eval_jaxpr/hqk,qhe->khe/dot_general | solution.py:86
  536.5 7.4 fusion.176
  545.8 7.7 bitcast_convert_fusion
  553.6 10.5 %convolution_bitcast_fusion = f32[3072,768]{1,0:T(8,128)} fusion(bf16[2,384,3072]{2,1,0:T(8,128)(2,1)} %get-tuple-element.122, bf16[2,384,768]{2,1,0:T(8,128)(2,1)} %param.33), kind=kOutput, calls=%fused_computation.140 | convolution fusion | flops 3623878656 | bytes 15335424 | tf_op jit(solution)/shard_map/rlf,rld->fd/dot_general | solution.py:155
  564.1 9.2 convolution_bitcast_fusion.1
  574.0 8.8 add_convert_fusion.3
  583.3 21.5 %psum.87 = bf16[2,192]{1,0:T(2,128)(2,1)S(1)} all-reduce(bf16[2,192]{1,0:T(2,128)(2,1)S(1)} %slice_reduce_fusion), channel_id=1, replica_groups=mesh['dp'=8,'th'=2,'tw'=2] {'dp'}, use_global_device_ids=true, to_apply=%region_29.30 | all-reduce | flops 384 | bytes 1536 | tf_op jit(solution)/shard_map/psum | solution.py:190
  605.3 20.9 %all-reduce.8.cloned.1.call-done = (bf16[3,768,192]{1,2,0:T(8,128)(2,1)}, bf16[192,768]{1,0:T(8,128)(2,1)}) async-done(((bf16[3,768,192]{1,2,0:T(8,128)(2,1)}, bf16[192,768]{1,0:T(8,128)(2,1)}), (bf16[3,768,192]{1,2,0:T(8,128)(2,1)}, bf16[192,768]{1,0:T(8,128)(2,1)})) %all-reduce.8.cloned.1.call-update) | async-done | bytes 1179664 | tf_op jit(solution)/shard_map/psum | solution.py:189
  628.0 2.5 convert_element_type.154
  630.5 45.2 %reduce-scatter.5.cloned.1.call-done = bf16[2,384,768]{2,1,0:T(8,128)(2,1)} async-done(((bf16[2,1536,768]{2,1,0:T(8,128)(2,1)}), bf16[2,384,768]{2,1,0:T(8,128)(2,1)}) %reduce-scatter.5.cloned.1.call-update) | async-done | bytes 1179664 | tf_op jit(solution)/shard_map/reduce_scatter | solution.py:183
  678.0 2.7 fusion.165
  680.8 3.0 convert_reduce_fusion.3
  683.8 42.5 %all-reduce = (f32[768]{0:T(1024)}, f32[768]{0:T(1024)}, f32[768]{0:T(1024)}, f32[768]{0:T(1024)}, f32[768]{0:T(1024)}, /*index=5*/f32[3072]{0:T(1024)}, f32[768]{0:T(1024)}) all-reduce(f32[768]{0:T(1024)S(1)} %get-tuple-element.81, f32[768]{0:T(1024)S(1)} %get-tuple-element.85, ...), channel_id=1, replica_groups=mesh['dp'=8,'th'=2,'tw'=2] {'dp','th','tw'}, use_global_device_ids=true, to_apply=%region_24.25 | all-reduce | flops 7680 | bytes 61440 | tf_op jit(solution)/shard_map/psum | solution.py:193
  726.3 262.5 %all-reduce.6.cloned.1.call-done = (f32[768,3072]{1,0:T(8,128)}, f32[3072,768]{1,0:T(8,128)}) async-done(((f32[768,3072]{1,0:T(8,128)}, f32[3072,768]{1,0:T(8,128)}), (f32[768,3072]{1,0:T(8,128)}, f32[3072,768]{1,0:T(8,128)})) %all-reduce.6.cloned.1.call-update) | async-done | bytes 18874384 | tf_op jit(solution)/shard_map/psum | solution.py:193
  988.8 8.8 copy.64
  997.6 3.7 copy.65
  (223 shorter events, 78.3 us)
Async XLA Ops:
  7.2 50.8 %copy-start = (bf16[3,768,192]{1,2,0:T(8,128)(2,1)S(1)}, bf16[3,768,192]{1,2,0:T(8,128)(2,1)}, u32[]{:S(2)}) copy-start(bf16[3,768,192]{1,2,0:T(8,128)(2,1)} %param.23) | copy-start | bytes 2654212
  7.2 172.0 %reduce-scatter.3.cloned.1.call-start = ((), (), s32[]{:S(2)}) async-start(), calls=%async_computation.2 | async-start | bytes 5898240 | tf_op jit(solution)/shard_map/reduce_scatter | solution.py:138
  8.8 5.2 copy-start.33
  8.8 35.7 %copy-start.49 = (f32[2,192]{1,0:T(2,128)S(1)}, f32[2,192]{1,0:T(2,128)}, u32[]{:S(2)}) copy-start(f32[2,192]{1,0:T(2,128)} %param.24) | copy-start | bytes 4612
  11.2 5.2 copy-start.38
  14.0 28.9 %collective-permute-start = (bf16[2,384,768]{2,1,0:T(8,128)(2,1)S(1)}, bf16[2,384,768]{2,1,0:T(8,128)(2,1)S(1)}, u32[]{:S(2)}, u32[]{:S(2)}) collective-permute-start(bf16[2,384,768]{2,1,0:T(8,128)(2,1)S(1)} %get-tuple-element.125), channel_id=1, source_target_pairs={{0,3},{1,0},{2,1},{3,2},{4,7},{5,4},{6,5},{7,6},{8,11},{9,8},{10,9... | collective-permute-start | bytes 3538952 | tf_op jit(solution)/shard_map/ppermute | solution.py:127
  44.5 4.9 collective-permute-start.1
  58.0 6.9 copy-start.17
  58.0 6.9 copy-start.21
  124.2 5.0 copy-start.18
  124.2 55.0 %copy-start.5 = (bf16[2,384,768]{2,1,0:T(8,128)(2,1)S(1)}, bf16[2,384,768]{2,1,0:T(8,128)(2,1)}, u32[]{:S(2)}) copy-start(bf16[2,384,768]{2,1,0:T(8,128)(2,1)} %param.19) | copy-start | bytes 3538948
  124.2 55.0 %copy-start.22 = (f32[768]{0:T(1024)S(1)}, f32[768]{0:T(1024)}, u32[]{:S(2)}) copy-start(f32[768]{0:T(1024)} %param.26) | copy-start | bytes 9220
  129.1 53.8 %copy-start.26 = (f32[768]{0:T(1024)S(1)}, f32[768]{0:T(1024)}, u32[]{:S(2)}) copy-start(f32[768]{0:T(1024)} %param.27) | copy-start | bytes 9220
  129.1 53.8 %copy-start.31 = (f32[768]{0:T(1024)S(1)}, f32[768]{0:T(1024)}, u32[]{:S(2)}) copy-start(f32[768]{0:T(1024)} %param.28) | copy-start | bytes 9220
  129.1 53.8 %copy-start.46 = (f32[3072]{0:T(1024)S(1)}, f32[3072]{0:T(1024)}, u32[]{:S(2)}) copy-start(f32[3072]{0:T(1024)} %param.30) | copy-start | bytes 36868
  129.2 149.5 %all-gather.2.cloned.1.call-start = ((), (), s32[]{:S(2)}) async-start(), calls=%async_computation.3 | async-start | bytes 5898240 | tf_op jit(solution)/shard_map/all_gather | solution.py:172
  179.2 3.8 copy-start.7
  181.0 57.3 %copy-start.24 = (f32[2,384]{1,0:T(2,128)}, f32[2,384]{1,0:T(2,128)S(1)}, u32[]{:S(2)}) copy-start(f32[2,384]{1,0:T(2,128)S(1)} %broadcast_multiply_fusion) | copy-start | bytes 9220
  183.0 55.3 %copy-start.28 = (f32[2,384]{1,0:T(2,128)}, f32[2,384]{1,0:T(2,128)S(1)}, u32[]{:S(2)}) copy-start(f32[2,384]{1,0:T(2,128)S(1)} %fusion.185) | copy-start | bytes 9220
  192.2 23.5 %copy-start.15 = (bf16[2,384,768]{2,1,0:T(8,128)(2,1)S(1)}, bf16[2,384,768]{2,1,0:T(8,128)(2,1)}, u32[]{:S(2)}) copy-start(bf16[2,384,768]{2,1,0:T(8,128)(2,1)} %param.33) | copy-start | bytes 3538948
  236.3 4.8 copy-start.9
  236.3 4.8 copy-start.36
  238.3 40.4 %copy-start.30 = (bf16[192,768]{1,0:T(8,128)(2,1)S(1)}, bf16[192,768]{1,0:T(8,128)(2,1)}, u32[]{:S(2)}) copy-start(bf16[192,768]{1,0:T(8,128)(2,1)} %param.25) | copy-start | bytes 884740
  238.3 45.4 %copy-start.40 = (f32[2,384]{1,0:T(2,128)}, f32[2,384]{1,0:T(2,128)S(1)}, u32[]{:S(2)}) copy-start(f32[2,384]{1,0:T(2,128)S(1)} %negate_multiply_fusion.2) | copy-start | bytes 9220
  241.1 385.1 %all-reduce.8.cloned.1.call-start = ((), (), s32[]{:S(2)}) async-start(), calls=%async_computation.6 | async-start | bytes 2359296 | tf_op jit(solution)/shard_map/psum | solution.py:189
  287.1 4.9 copy-start.12
  291.0 3.6 copy-start.2
  297.1 7.7 copy-start.4
  299.6 4.3 copy-start.3
  394.8 14.0 %copy-start.13 = (bf16[3,64,512]{2,1,0:T(8,128)(2,1)S(1)}, bf16[3,64,512]{2,1,0:T(8,128)(2,1)}, u32[]{:S(2)}) copy-start(bf16[3,64,512]{2,1,0:T(8,128)(2,1)} %fusion.382) | copy-start | bytes 589828 | tf_op jit(solution)/shard_map/while
  394.8 14.0 %copy-start.14 = (bf16[3,64,512]{2,1,0:T(8,128)(2,1)S(1)}, bf16[3,64,512]{2,1,0:T(8,128)(2,1)}, u32[]{:S(2)}) copy-start(bf16[3,64,512]{2,1,0:T(8,128)(2,1)} %fusion.383) | copy-start | bytes 589828 | tf_op jit(solution)/shard_map/while
  413.2 4.9 copy-start.12
  417.1 3.6 copy-start.2
  423.2 7.7 copy-start.4
  425.7 4.3 copy-start.3
  520.9 14.0 %copy-start.13 = (bf16[3,64,512]{2,1,0:T(8,128)(2,1)S(1)}, bf16[3,64,512]{2,1,0:T(8,128)(2,1)}, u32[]{:S(2)}) copy-start(bf16[3,64,512]{2,1,0:T(8,128)(2,1)} %fusion.382) | copy-start | bytes 589828 | tf_op jit(solution)/shard_map/while
  520.9 14.0 %copy-start.14 = (bf16[3,64,512]{2,1,0:T(8,128)(2,1)S(1)}, bf16[3,64,512]{2,1,0:T(8,128)(2,1)}, u32[]{:S(2)}) copy-start(bf16[3,64,512]{2,1,0:T(8,128)(2,1)} %fusion.383) | copy-start | bytes 589828 | tf_op jit(solution)/shard_map/while
  536.5 7.4 copy-start.19
  536.5 7.4 copy-start.50
  545.7 130.0 %reduce-scatter.5.cloned.1.call-start = ((), (), s32[]{:S(2)}) async-start(), calls=%async_computation.4 | async-start | bytes 5898240 | tf_op jit(solution)/shard_map/reduce_scatter | solution.py:183
  553.4 435.4 %all-reduce.6.cloned.1.call-start = ((), (), s32[]{:S(2)}) async-start(), calls=%async_computation.5 | async-start | bytes 37748736 | tf_op jit(solution)/shard_map/psum | solution.py:193
  553.5 10.6 %copy-start.6 = (bf16[2,384,768]{2,1,0:T(8,128)(2,1)S(1)}, bf16[2,384,768]{2,1,0:T(8,128)(2,1)}, u32[]{:S(2)}) copy-start(bf16[2,384,768]{2,1,0:T(8,128)(2,1)} %param.19) | copy-start | bytes 3538948
  553.5 10.6 %copy-start.8 = (bf16[2,384,768]{2,1,0:T(8,128)(2,1)S(1)}, bf16[2,384,768]{2,1,0:T(8,128)(2,1)}, u32[]{:S(2)}) copy-start(bf16[2,384,768]{2,1,0:T(8,128)(2,1)} %reduce-scatter.3.cloned.1.call-done) | copy-start | bytes 3538948
  553.5 10.5 %copy-start.23 = (f32[768]{0:T(1024)S(1)}, f32[768]{0:T(1024)}, u32[]{:S(2)}) copy-start(f32[768]{0:T(1024)} %param.26) | copy-start | bytes 9220
  553.5 10.5 %copy-start.25 = (f32[2,384]{1,0:T(2,128)S(1)}, f32[2,384]{1,0:T(2,128)}, u32[]{:S(2)}) copy-start(f32[2,384]{1,0:T(2,128)} %copy-done.24) | copy-start | bytes 9220
  553.5 10.5 %copy-start.27 = (f32[768]{0:T(1024)S(1)}, f32[768]{0:T(1024)}, u32[]{:S(2)}) copy-start(f32[768]{0:T(1024)} %param.27) | copy-start | bytes 9220
  553.6 10.5 %copy-start.29 = (f32[2,384]{1,0:T(2,128)S(1)}, f32[2,384]{1,0:T(2,128)}, u32[]{:S(2)}) copy-start(f32[2,384]{1,0:T(2,128)} %copy-done.28) | copy-start | bytes 9220
  553.6 10.5 %copy-start.32 = (f32[768]{0:T(1024)S(1)}, f32[768]{0:T(1024)}, u32[]{:S(2)}) copy-start(f32[768]{0:T(1024)} %param.28) | copy-start | bytes 9220
  574.0 8.8 copy-start.20
  582.8 92.9 %copy-start.34 = (f32[2,384]{1,0:T(2,128)S(1)}, f32[2,384]{1,0:T(2,128)}, u32[]{:S(2)}) copy-start(f32[2,384]{1,0:T(2,128)} %copy-done.33) | copy-start | bytes 9220
  582.8 92.9 %copy-start.35 = (f32[768]{0:T(1024)S(1)}, f32[768]{0:T(1024)}, u32[]{:S(2)}) copy-start(f32[768]{0:T(1024)} %param.21) | copy-start | bytes 9220
  582.8 95.1 %copy-start.43 = (f32[2,384]{1,0:T(2,128)S(1)}, f32[2,384]{1,0:T(2,128)}, u32[]{:S(2)}) copy-start(f32[2,384]{1,0:T(2,128)} %copy-done.42) | copy-start | bytes 9220
  582.8 95.2 %copy-start.39 = (f32[2,384]{1,0:T(2,128)S(1)}, f32[2,384]{1,0:T(2,128)}, u32[]{:S(2)}) copy-start(f32[2,384]{1,0:T(2,128)} %copy-done.38) | copy-start | bytes 9220
  583.2 97.5 %copy-start.37 = (f32[2,384]{1,0:T(2,128)S(1)}, f32[2,384]{1,0:T(2,128)}, u32[]{:S(2)}) copy-start(f32[2,384]{1,0:T(2,128)} %copy-done.36) | copy-start | bytes 9220
  583.3 97.5 %copy-start.41 = (f32[2,384]{1,0:T(2,128)S(1)}, f32[2,384]{1,0:T(2,128)}, u32[]{:S(2)}) copy-start(f32[2,384]{1,0:T(2,128)} %copy-done.40) | copy-start | bytes 9220
  675.7 5.1 copy-start.10
  675.7 5.1 copy-start.11
  675.7 5.1 copy-start.16
  680.7 3.1 copy-start.44
  680.7 3.1 copy-start.45
  680.7 3.1 copy-start.47
  988.8 8.8 slice-start
  988.8 8.8 slice-start.1
  988.8 8.8 slice-start.2
  (5 other events, 10.0 us)
Sparse Core Ops, SparseCore 0:
  129.3 49.8 reduce-scatter.2
  241.2 37.4 all-gather.1
  545.8 80.2 all-reduce.7
  628.5 47.1 reduce-scatter.4
  683.7 305.1 all-reduce.5
